TPU v7x, 32 devices: a whole 2x2x4 slice. The times are simulated.
32 devices in a mesh: seq: 4 (over y, core), user: 8 (over z, x).
Axes of the slice: x: 2, y: 2, z: 4, core: 2. Of those that a mesh axis runs over, the one named last changes fastest.
Arguments:
- history: bfloat16 [8, 2048, 256], P('user', 'seq'), may hold values from -6 to 6
- cotangent: bfloat16 [8, 2048, 256], P('user', 'seq'), may hold values from -6 to 6
- weights: bfloat16 [4, 3, 256, 256], replicated, may hold values from -0.21875 to 0.21875
- ln_gain: float32 [4, 256], replicated, may hold values from 0.1 to 1.9
- conv_bias: float32 [4, 256], replicated, may hold values from -3 to 3
- pooled_grad: bfloat16 [8, 64, 128], P('user', 'seq'), may hold values from -6 to 6
- table_owner: int32 [64], P('seq'), may hold values from 0 to 7, as said below
- row_ids: int32 [8, 64], P('user', 'seq'), may hold values from 0 to 999999
Outputs:
- d_history: bfloat16 [8, 2048, 256], P('user', 'seq')
- grad_weights: float32 [4, 3, 256, 256], replicated
- grad_gain: float32 [4, 256], replicated
- grad_bias: float32 [4, 256], replicated
- table_grad: float32 [64, 8, 128], P(('seq', 'user'))
Inputs may be any that keep to these rules, and one draw needn't show every extreme that they name: `table_owner`: within each block of 16 consecutive tables, every user index owns exactly 2 tables.
All inputs are finite; a program needn't handle non-finite values.
Results may differ from a plain program's by a relative error of at most 0.0095.
Values may be sent and summed in bfloat16 or wider, within the bound.
A program may use at most 64 MiB of HBM per device.

v0:
```python
import math
import jax
import jax.numpy as jnp
from jax import lax
from jax.sharding import PartitionSpec as P

TAPS = 3
LAYERS = 4
epsilon = 1e-05


def passed_along(block, axis, distance):
    devices = range(lax.axis_size(axis))
    route = [(i - distance, i) for i in devices if i - distance in devices]
    return lax.ppermute(block, axis, route)


def gelu_tanh(values):
    return jax.nn.gelu(values, approximate=True)


def gelu_slope(values, upstream):
    return jax.vjp(gelu_tanh, values)[1](upstream)[0]


def normalize(resid_field):
    center = resid_field - jnp.mean(resid_field, -1, keepdims=True)
    inverse = lax.rsqrt(jnp.mean(center * center, -1, keepdims=True) + epsilon)
    return (center * inverse, inverse)


def dilated(padded, kernel, shift_bias, dilation):
    user_count, total_len, channels = padded.shape
    out_len = total_len - (TAPS - 1) * dilation
    result = jnp.zeros((user_count * out_len, kernel.shape[2]), jnp.float32) + shift_bias
    for tap_index in range(TAPS):
        offset = (TAPS - 1 - tap_index) * dilation
        window = padded[:, offset : offset + out_len].reshape(user_count * out_len, channels)
        result = result + jnp.dot(window, kernel[tap_index], preferred_element_type=jnp.float32)
    return result.reshape(user_count, out_len, kernel.shape[2])


def coalesce(pieces):
    got_rows, got_ids = pieces
    per_owner = got_rows.shape[2]
    flat_rows = got_rows.reshape(got_rows.shape[0], per_owner, got_rows.shape[3])
    key_grid = got_ids.reshape(got_ids.shape[0], per_owner).T
    matches = (key_grid[:, :, None] == key_grid[:, None, :]).astype(jnp.bfloat16)
    return jnp.einsum("tuv,vte->tue", matches, flat_rows, preferred_element_type=jnp.float32)


def body(history, cotangent, weights, ln_gain, conv_bias, pooled_grad, table_owner, row_ids):
    user_count, length, channels = history.shape
    row_count = user_count * length
    stored = []
    resid_field = history.astype(jnp.float32)
    for layer_num in range(LAYERS):
        dilation = 2**layer_num
        lookback = (TAPS - 1) * dilation
        normed, inverse = normalize(resid_field)
        hidden = gelu_tanh(normed * ln_gain[layer_num]).astype(jnp.bfloat16)
        border = passed_along(hidden[:, length - lookback :], "seq", 1)
        padded = jnp.concatenate([border, hidden], 1)
        stored.append((resid_field, padded))
        resid_field = resid_field + dilated(
            padded, weights[layer_num], conv_bias[layer_num], dilation
        )
    grad_flow = cotangent.astype(jnp.float32)
    weight_terms = [None] * LAYERS
    gain_terms = [None] * LAYERS
    bias_terms = [None] * LAYERS
    for layer_num in reversed(range(LAYERS)):
        dilation = 2**layer_num
        lookback = (TAPS - 1) * dilation
        field_in, padded = stored[layer_num]
        flow_half = grad_flow.astype(jnp.bfloat16)
        flow_flat = flow_half.reshape(row_count, channels)
        bias_terms[layer_num] = jnp.sum(grad_flow, (0, 1))
        tap_terms = []
        for tap_index in range(TAPS):
            offset = lookback - tap_index * dilation
            window = padded[:, offset : offset + length].reshape(row_count, channels)
            tap_terms.append(
                lax.dot_general(
                    window, flow_flat, (((0,), (0,)), ((), ())), preferred_element_type=jnp.float32
                )
            )
        weight_terms[layer_num] = jnp.stack(tap_terms)
        future = passed_along(flow_half[:, :lookback], "seq", -1)
        extended = jnp.concatenate([flow_half, future], 1)
        backward = jnp.zeros((row_count, channels), jnp.float32)
        for tap_index in range(TAPS):
            offset = tap_index * dilation
            window = extended[:, offset : offset + length].reshape(row_count, channels)
            backward = backward + lax.dot_general(
                window,
                weights[layer_num, tap_index],
                (((1,), (1,)), ((), ())),
                preferred_element_type=jnp.float32,
            )
        normed, inverse = normalize(field_in)
        slopes = gelu_slope(
            normed * ln_gain[layer_num], backward.reshape(user_count, length, channels)
        )
        gain_terms[layer_num] = jnp.sum(slopes * normed, (0, 1))
        scaled = slopes * ln_gain[layer_num]
        grad_flow = grad_flow + inverse * (
            scaled
            - jnp.mean(scaled, -1, keepdims=True)
            - normed * jnp.mean(scaled * normed, -1, keepdims=True)
        )
    weight_local = jnp.stack(weight_terms)
    gain_local = jnp.stack(gain_terms)
    bias_local = jnp.stack(bias_terms)
    weight_total, gain_total, bias_total = lax.psum(
        (weight_local, gain_local, bias_local), ("seq", "user")
    )
    factor = 1.0 / math.sqrt(user_count * lax.axis_size("user") * length * lax.axis_size("seq"))
    listing = jnp.argsort(table_owner, stable=True)
    per_owner = listing.shape[0] // lax.axis_size("user")
    send_rows = jnp.take(pooled_grad, listing, axis=1).reshape(
        user_count, lax.axis_size("user"), per_owner, pooled_grad.shape[2]
    )
    send_ids = jnp.take(row_ids, listing, axis=1).reshape(
        user_count, lax.axis_size("user"), per_owner
    )
    table_grad = coalesce(
        (
            lax.all_to_all(send_rows, "user", split_axis=1, concat_axis=0, tiled=True),
            lax.all_to_all(send_ids, "user", split_axis=1, concat_axis=0, tiled=True),
        )
    )
    return (
        grad_flow.astype(jnp.bfloat16),
        weight_total * factor,
        gain_total * factor,
        bias_total * factor,
        table_grad,
    )


def solution(mesh):
    in_specs = (
        P("user", "seq", None),
        P("user", "seq", None),
        P(),
        P(),
        P(),
        P("user", "seq", None),
        P("seq"),
        P("user", "seq"),
    )
    out_specs = (P("user", "seq", None), P(), P(), P(), P(("seq", "user"), None, None))
    return jax.shard_map(body, mesh=mesh, in_specs=in_specs, out_specs=out_specs, check_vma=False)
```

profile of v0, /device:TPU:0, one launch (start us, length us, event | category | flops | bytes accessed | tf_op | source)
XLA Modules:
  0.0 236.2 jit_solution(5344520800691517173)
XLA Ops:
  7.2 0.8 fusion.190
  8.0 1.1 convert_reduce_fusion
  9.2 1.2 fusion.30
  10.3 1.3 fusion.21
  11.6 2.4 %collective-permute-start = (bf16[1,2,256]{2,1,0:T(2,128)(2,1)S(1)}, bf16[1,2,256]{2,1,0:T(2,128)(2,1)S(1)}, u32[]{:S(2)}, u32[]{:S(2)}) collective-permute-start(bf16[1,2,256]{2,1,0:T(2,128)(2,1)S(1)} %slice.220), channel_id=1, source_target_pairs={{0,8},{8,16},{16,24},{1,9},{9,17},{17,25},{2,10},{10,18},{18,26},{... | collective-permute-start | bytes 3080 | tf_op jit(solution)/shard_map/ppermute | solution.py:15
  14.0 0.7 slice.198
  14.7 1.3 collective-permute-start.3
  16.0 1.9 sort.17
  17.9 1.3 gather_fusion
  19.3 0.7 reshape.430
  19.9 6.6 %all-to-all-start = ((s32[1,8,2]{2,0,1:T(1,128)}), s32[1,8,2]{2,0,1:T(1,128)S(1)}, u32[]{:S(2)}, u32[]{:S(2)}) async-start(s32[1,8,2]{2,0,1:T(1,128)} %bitcast.75), calls=%async_computation | async-start | bytes 8192 | tf_op jit(solution)/shard_map/all_to_all | solution.py:130
  26.6 1.2 fusion.104
  27.8 1.2 convolution_add_fusion.16
  29.6 0.7 fusion.162
  30.3 0.7 constant_dynamic-update-slice_fusion.1
  31.0 2.0 all-to-all-done
  33.0 4.0 %all-to-all-start.1 = ((bf16[1,8,2,128]{3,2,0,1:T(2,128)(2,1)}), bf16[1,8,2,128]{3,2,0,1:T(2,128)(2,1)S(1)}, u32[]{:S(2)}, u32[]{:S(2)}) async-start(bf16[1,8,2,128]{3,2,0,1:T(2,128)(2,1)} %fusion.162), calls=%async_computation.1 | async-start | bytes 8192 | tf_op jit(solution)/shard_map/all_to_all | solution.py:129
  37.2 1.1 convolution_add_fusion.15
  38.3 1.3 fusion.192
  40.1 3.5 %collective-permute-start.1 = (bf16[1,4,256]{2,1,0:T(4,128)(2,1)S(1)}, bf16[1,4,256]{2,1,0:T(4,128)(2,1)S(1)}, u32[]{:S(2)}, u32[]{:S(2)}) collective-permute-start(bf16[1,4,256]{2,1,0:T(4,128)(2,1)S(1)} %slice.223), channel_id=1, source_target_pairs={{0,8},{8,16},{16,24},{1,9},{9,17},{17,25},{2,10},{10,18},{18,26},{... | collective-permute-start | bytes 6152 | tf_op jit(solution)/shard_map/ppermute | solution.py:15
  43.7 1.1 convolution_add_fusion.13
  44.8 1.1 convolution_add_fusion.12
  46.0 1.3 fusion.193
  47.8 4.5 %collective-permute-start.2 = (bf16[1,8,256]{2,1,0:T(8,128)(2,1)S(1)}, bf16[1,8,256]{2,1,0:T(8,128)(2,1)S(1)}, u32[]{:S(2)}, u32[]{:S(2)}) collective-permute-start(bf16[1,8,256]{2,1,0:T(8,128)(2,1)S(1)} %slice.226), channel_id=1, source_target_pairs={{0,8},{8,16},{16,24},{1,9},{9,17},{17,25},{2,10},{10,18},{18,26},{... | collective-permute-start | bytes 12296 | tf_op jit(solution)/shard_map/ppermute | solution.py:15
  52.3 1.1 convolution_add_fusion.10
  53.4 1.1 convolution_add_fusion.9
  54.6 1.2 fusion.194
  56.1 0.8 fusion.160
  56.9 0.6 constant_dynamic-update-slice_fusion
  57.5 1.2 convolution_add_fusion.7
  58.8 1.8 multiply_reduce_fusion
  61.0 0.9 copy-done.3
  62.8 1.3 collective-permute-start.4
  64.1 4.3 %collective-permute-start.7 = (bf16[1,16,256]{2,1,0:T(8,128)(2,1)S(1)}, bf16[1,16,256]{2,1,0:T(8,128)(2,1)S(1)}, u32[]{:S(2)}, u32[]{:S(2)}) collective-permute-start(bf16[1,16,256]{2,1,0:T(8,128)(2,1)S(1)} %slice.240), channel_id=1, source_target_pairs={{0,8},{8,16},{16,24},{1,9},{9,17},{17,25},{2,10},{10,18},{18,26},{... | collective-permute-start | bytes 24584 | tf_op jit(solution)/shard_map/ppermute | solution.py:15
  69.3 0.8 multiply_reduce_fusion.1
  71.1 1.3 collective-permute-start.5
  73.0 2.5 %collective-permute-done.5 = bf16[1,4,256]{2,1,0:T(4,128)(2,1)S(1)} collective-permute-done((bf16[1,4,256]{2,1,0:T(4,128)(2,1)S(1)}, bf16[1,4,256]{2,1,0:T(4,128)(2,1)S(1)}, u32[]{:S(2)}, u32[]{:S(2)}) %collective-permute-start.5) | collective-permute-done | bytes 2080 | tf_op jit(solution)/shard_map/ppermute | solution.py:15
  75.7 0.8 multiply_reduce_fusion.2
  77.5 1.5 collective-permute-start.6
  80.2 2.1 pad_maximum_fusion
  82.4 1.2 convolution_add_fusion.1
  83.6 1.7 fusion.29
  85.3 44.3 %all-reduce = (f32[4,256]{1,0:T(4,128)S(1)}, f32[4,256]{1,0:T(4,128)S(1)}) all-reduce(f32[4,256]{1,0:T(4,128)S(1)} %pad_maximum_fusion.8, f32[4,256]{1,0:T(4,128)S(1)} %pad_maximum_fusion.9), channel_id=1, replica_groups=mesh['seq'=4,'user'=8] {'seq','user'}, use_global_device_ids=true, to_apply=%region_21.0 | all-reduce | flops 2048 | bytes 16384 | tf_op jit(solution)/shard_map/psum | solution.py:115
  129.6 0.6 broadcast_multiply_fusion.2
  130.2 0.6 broadcast_multiply_fusion.1
  130.8 1.0 fusion.28
  131.8 93.8 %all-reduce.3.cloned.1.call-done = f32[4,3,256,256]{3,2,1,0:T(8,128)} async-done(((f32[4,3,256,256]{3,2,1,0:T(8,128)}), f32[4,3,256,256]{3,2,1,0:T(8,128)}) %all-reduce.3.cloned.1.call-update) | async-done | bytes 3145744 | tf_op jit(solution)/shard_map/psum | solution.py:115
  225.6 3.8 %broadcast_multiply_fusion = f32[4,3,256,256]{3,2,1,0:T(8,128)} fusion(f32[4,3,256,256]{3,2,1,0:T(8,128)} %all-reduce.3.cloned.1.call-done), kind=kLoop, calls=%fused_computation.3 | loop fusion | flops 786432 | bytes 6291456 | tf_op jit(solution)/shard_map/mul | solution.py:135
  (83 shorter events, 8.4 us)
Async XLA Ops:
  7.2 21.8 %copy-start = (bf16[1,16,128]{2,1,0:T(8,128)(2,1)S(1)}, bf16[1,16,128]{2,1,0:T(8,128)(2,1)}, u32[]{:S(2)}) copy-start(bf16[1,16,128]{2,1,0:T(8,128)(2,1)} %param.13) | copy-start | bytes 12292
  7.2 19.4 %copy-start.2 = (bf16[1,512,256]{2,1,0:T(8,128)(2,1)S(1)}, bf16[1,512,256]{2,1,0:T(8,128)(2,1)}, u32[]{:S(2)}) copy-start(bf16[1,512,256]{2,1,0:T(8,128)(2,1)} %param.9) | copy-start | bytes 786436
  7.2 19.4 %copy-start.4 = (f32[4,256]{1,0:T(4,128)S(1)}, f32[4,256]{1,0:T(4,128)}, u32[]{:S(2)}) copy-start(f32[4,256]{1,0:T(4,128)} %param.12) | copy-start | bytes 12292
  11.6 25.5 %collective-permute-start = (bf16[1,2,256]{2,1,0:T(2,128)(2,1)S(1)}, bf16[1,2,256]{2,1,0:T(2,128)(2,1)S(1)}, u32[]{:S(2)}, u32[]{:S(2)}) collective-permute-start(bf16[1,2,256]{2,1,0:T(2,128)(2,1)S(1)} %slice.220), channel_id=1, source_target_pairs={{0,8},{8,16},{16,24},{1,9},{9,17},{17,25},{2,10},{10,18},{18,26},{... | collective-permute-start | bytes 3080 | tf_op jit(solution)/shard_map/ppermute | solution.py:15
  14.7 42.2 %collective-permute-start.3 = (bf16[1,16,256]{2,1,0:T(8,128)(2,1)S(1)}, bf16[1,16,256]{2,1,0:T(8,128)(2,1)S(1)}, u32[]{:S(2)}, u32[]{:S(2)}) collective-permute-start(bf16[1,16,256]{2,1,0:T(8,128)(2,1)S(1)} %slice.198), channel_id=1, source_target_pairs={{8,0},{16,8},{24,16},{9,1},{17,9},{25,17},{10,2},{18,10},{26,18},{... | collective-permute-start | bytes 24584 | tf_op jit(solution)/shard_map/ppermute | solution.py:15
  19.9 13.0 %all-to-all-start = ((s32[1,8,2]{2,0,1:T(1,128)}), s32[1,8,2]{2,0,1:T(1,128)S(1)}, u32[]{:S(2)}, u32[]{:S(2)}) async-start(s32[1,8,2]{2,0,1:T(1,128)} %bitcast.75), calls=%async_computation | async-start | bytes 8192 | tf_op jit(solution)/shard_map/all_to_all | solution.py:130
  27.8 10.5 %copy-start.1 = (bf16[1,512,256]{2,1,0:T(8,128)(2,1)S(1)}, bf16[1,512,256]{2,1,0:T(8,128)(2,1)}, u32[]{:S(2)}) copy-start(bf16[1,512,256]{2,1,0:T(8,128)(2,1)} %param.8) | copy-start | bytes 786436
  33.0 23.1 %all-to-all-start.1 = ((bf16[1,8,2,128]{3,2,0,1:T(2,128)(2,1)}), bf16[1,8,2,128]{3,2,0,1:T(2,128)(2,1)S(1)}, u32[]{:S(2)}, u32[]{:S(2)}) async-start(bf16[1,8,2,128]{3,2,0,1:T(2,128)(2,1)} %fusion.162), calls=%async_computation.1 | async-start | bytes 8192 | tf_op jit(solution)/shard_map/all_to_all | solution.py:129
  37.0 188.6 %all-reduce.3.cloned.1.call-start = ((), (), s32[]{:S(2)}) async-start(), calls=%async_computation.2 | async-start | bytes 6291456 | tf_op jit(solution)/shard_map/psum | solution.py:115
  40.1 4.6 %collective-permute-start.1 = (bf16[1,4,256]{2,1,0:T(4,128)(2,1)S(1)}, bf16[1,4,256]{2,1,0:T(4,128)(2,1)S(1)}, u32[]{:S(2)}, u32[]{:S(2)}) collective-permute-start(bf16[1,4,256]{2,1,0:T(4,128)(2,1)S(1)} %slice.223), channel_id=1, source_target_pairs={{0,8},{8,16},{16,24},{1,9},{9,17},{17,25},{2,10},{10,18},{18,26},{... | collective-permute-start | bytes 6152 | tf_op jit(solution)/shard_map/ppermute | solution.py:15
  47.8 5.6 %collective-permute-start.2 = (bf16[1,8,256]{2,1,0:T(8,128)(2,1)S(1)}, bf16[1,8,256]{2,1,0:T(8,128)(2,1)S(1)}, u32[]{:S(2)}, u32[]{:S(2)}) collective-permute-start(bf16[1,8,256]{2,1,0:T(8,128)(2,1)S(1)} %slice.226), channel_id=1, source_target_pairs={{0,8},{8,16},{16,24},{1,9},{9,17},{17,25},{2,10},{10,18},{18,26},{... | collective-permute-start | bytes 12296 | tf_op jit(solution)/shard_map/ppermute | solution.py:15
  60.5 1.4 copy-start.3
  62.8 6.3 %collective-permute-start.4 = (bf16[1,8,256]{2,1,0:T(8,128)(2,1)S(1)}, bf16[1,8,256]{2,1,0:T(8,128)(2,1)S(1)}, u32[]{:S(2)}, u32[]{:S(2)}) collective-permute-start(bf16[1,8,256]{2,1,0:T(8,128)(2,1)S(1)} %slice.231), channel_id=1, source_target_pairs={{8,0},{16,8},{24,16},{9,1},{17,9},{25,17},{10,2},{18,10},{26,18},{... | collective-permute-start | bytes 12296 | tf_op jit(solution)/shard_map/ppermute | solution.py:15
  64.1 15.5 %collective-permute-start.7 = (bf16[1,16,256]{2,1,0:T(8,128)(2,1)S(1)}, bf16[1,16,256]{2,1,0:T(8,128)(2,1)S(1)}, u32[]{:S(2)}, u32[]{:S(2)}) collective-permute-start(bf16[1,16,256]{2,1,0:T(8,128)(2,1)S(1)} %slice.240), channel_id=1, source_target_pairs={{0,8},{8,16},{16,24},{1,9},{9,17},{17,25},{2,10},{10,18},{18,26},{... | collective-permute-start | bytes 24584 | tf_op jit(solution)/shard_map/ppermute | solution.py:15
  71.1 4.4 %collective-permute-start.5 = (bf16[1,4,256]{2,1,0:T(4,128)(2,1)S(1)}, bf16[1,4,256]{2,1,0:T(4,128)(2,1)S(1)}, u32[]{:S(2)}, u32[]{:S(2)}) collective-permute-start(bf16[1,4,256]{2,1,0:T(4,128)(2,1)S(1)} %slice.234), channel_id=1, source_target_pairs={{8,0},{16,8},{24,16},{9,1},{17,9},{25,17},{10,2},{18,10},{26,18},{... | collective-permute-start | bytes 6152 | tf_op jit(solution)/shard_map/ppermute | solution.py:15
  77.5 4.9 %collective-permute-start.6 = (bf16[1,2,256]{2,1,0:T(2,128)(2,1)S(1)}, bf16[1,2,256]{2,1,0:T(2,128)(2,1)S(1)}, u32[]{:S(2)}, u32[]{:S(2)}) collective-permute-start(bf16[1,2,256]{2,1,0:T(2,128)(2,1)S(1)} %slice.237), channel_id=1, source_target_pairs={{8,0},{16,8},{24,16},{9,1},{17,9},{25,17},{10,2},{18,10},{26,18},{... | collective-permute-start | bytes 3080 | tf_op jit(solution)/shard_map/ppermute | solution.py:15
Sparse Core Ops, SparseCore 0:
  82.4 143.1 all-reduce.2
where the time goes:
time: 237 us; the launch traced here: 236 us
  waiting for transfers between devices  98.4 us (42%)
  blocking collectives  44.3 us (19%)
  starting transfers between devices  30.8 us (13%)
  matrix products  24.5 us (10%)
  other arithmetic  17.1 us (7%)
  between operations  14.6 us (6%)
  local copies, waits for them, and re-layouts  6.56 us (3%)
    psum x1, waiting for transfers between devices, body(): lax.psum((weight_local, gain_local, bias_local), ('seq', 'user'))  93.8 us
    psum x1, blocking collectives, body(): lax.psum((weight_local, gain_local, bias_local), ('seq', 'user'))  44.3 us
    ppermute x8, starting transfers between devices, passed_along(): return lax.ppermute(block, axis, route)  20.1 us
    dot_general x9, matrix products, dilated(): jnp.dot(window, kernel[tap_index], preferred_element_type=jnp.float32)  10.6 us
    dot_general x12, matrix products, body(): lax.dot_general(window, weights[layer_num, tap_index], (((1,), (1,)), (()...  9.9 us
    all_to_all x1, starting transfers between devices, body(): lax.all_to_all(send_ids, 'user', split_axis=1, concat_axis=0, tiled=True)  6.62 us
  transfers between devices with their start and end apart: 11, of which 4 were waited for; matrix products, arithmetic and copies ran while one was open for 14% of the time, Pallas kernels for 0%

commit v1 on v0

--- a/solution.py
+++ b/solution.py
@@ -113,7 +113,7 @@
     gain_local = jnp.stack(gain_terms)
     bias_local = jnp.stack(bias_terms)
     weight_total, gain_total, bias_total = lax.psum(
-        (weight_local, gain_local, bias_local), ("seq", "user")
+        lax.psum((weight_local, gain_local, bias_local), "user"), "seq"
     )
     factor = 1.0 / math.sqrt(user_count * lax.axis_size("user") * length * lax.axis_size("seq"))
     listing = jnp.argsort(table_owner, stable=True)

time: 237 us -> 266 us (1.12)
  waiting for transfers between devices: 98.4 us -> 160 us
  blocking collectives: 44.3 us -> 26.4 us
  matrix products: 24.5 us -> 12.6 us
    psum x1 -> x2, waiting for transfers between devices: 93.8 us -> 144 us  [the longest x1 103 us: body(): lax.psum((weight_local, gain_local, bias_local), 'user')]
    psum x1 -> x2, blocking collectives: 44.3 us -> 26.4 us  [the longest x1 19.7 us: body(): lax.psum((weight_local, gain_local, bias_local), 'user')]
    dot_general x9, matrix products: 10.6 us -> 2.42 us  [dilated(): jnp.dot(window, kernel[tap_index], preferred_element_type=jnp.float32)]
    all_to_all x1, waiting for transfers between devices: 0.01 us -> 6.44 us  [body(): lax.all_to_all(send_rows, 'user', split_axis=1, concat_axis=0, tiled=True)]
    dot_general x12, matrix products: 9.9 us -> 6.21 us  [body(): lax.dot_general(window, weights[layer_num, tap_index], (((1,), (1,)), (()...]
    all_to_all x1, waiting for transfers between devices: 1.96 us -> 5.31 us  [body(): lax.all_to_all(send_ids, 'user', split_axis=1, concat_axis=0, tiled=True)]
  transfers between devices with their start and end apart: 11 -> 12, of which waited for: 4 -> 7; matrix products, arithmetic and copies ran while one was open for 14% -> 8% of each run, Pallas kernels for 0% -> 0%
where the time goes in v1:
time: 266 us; the launch traced here: 265 us
  waiting for transfers between devices  160 us (60%)
  starting transfers between devices  30.2 us (11%)
  blocking collectives  26.4 us (10%)
  other arithmetic  16.5 us (6%)
  between operations  14.7 us (6%)
  matrix products  12.6 us (5%)
  local copies, waits for them, and re-layouts  5.57 us (2%)
    psum x1, waiting for transfers between devices, body(): lax.psum((weight_local, gain_local, bias_local), 'user')  103 us
    psum x1, waiting for transfers between devices, body(): lax.psum(lax.psum((weight_local, gain_local, bias_local), 'user'), 'seq')  40.3 us
    ppermute x8, starting transfers between devices, passed_along(): return lax.ppermute(block, axis, route)  21 us
    psum x1, blocking collectives, body(): lax.psum((weight_local, gain_local, bias_local), 'user')  19.7 us
    psum x1, blocking collectives, body(): lax.psum(lax.psum((weight_local, gain_local, bias_local), 'user'), 'seq')  6.77 us
    all_to_all x1, waiting for transfers between devices, body(): lax.all_to_all(send_rows, 'user', split_axis=1, concat_axis=0, tiled=True)  6.44 us
    dot_general x12, matrix products, body(): lax.dot_general(window, weights[layer_num, tap_index], (((1,), (1,)), (()...  6.21 us
    all_to_all x1, starting transfers between devices, body(): lax.all_to_all(send_ids, 'user', split_axis=1, concat_axis=0, tiled=True)  5.81 us
  transfers between devices with their start and end apart: 12, of which 7 were waited for; matrix products, arithmetic and copies ran while one was open for 8% of the time, Pallas kernels for 0%

profile of v1, /device:TPU:0, one launch (start us, length us, event | category | flops | bytes accessed | tf_op | source)
XLA Modules:
  0.0 265.4 jit_solution(15766958914851045870)
XLA Ops:
  7.2 0.9 fusion.190
  8.1 1.1 convert_reduce_fusion
  9.2 1.2 fusion.30
  10.4 1.3 fusion.21
  11.7 2.4 collective-permute-start
  14.1 0.7 slice.198
  14.8 1.3 collective-permute-start.3
  16.1 0.8 fusion.191
  16.9 1.2 fusion.104
  18.7 0.4 copy-done.2
  19.1 0.3 fusion.192
  20.0 5.2 %collective-permute-start.1 = (bf16[1,4,256]{2,1,0:T(4,128)(2,1)S(1)}, bf16[1,4,256]{2,1,0:T(4,128)(2,1)S(1)}, u32[]{:S(2)}, u32[]{:S(2)}) collective-permute-start(bf16[1,4,256]{2,1,0:T(4,128)(2,1)S(1)} %slice.223), channel_id=1, source_target_pairs={{0,8},{8,16},{16,24},{1,9},{9,17},{17,25},{2,10},{10,18},{18,26},{... | collective-permute-start | bytes 6152 | tf_op jit(solution)/shard_map/ppermute | solution.py:15
  25.4 0.6 collective-permute-done.1
  26.2 0.4 fusion.193
  27.2 3.5 %collective-permute-start.2 = (bf16[1,8,256]{2,1,0:T(8,128)(2,1)S(1)}, bf16[1,8,256]{2,1,0:T(8,128)(2,1)S(1)}, u32[]{:S(2)}, u32[]{:S(2)}) collective-permute-start(bf16[1,8,256]{2,1,0:T(8,128)(2,1)S(1)} %slice.226), channel_id=1, source_target_pairs={{0,8},{8,16},{16,24},{1,9},{9,17},{17,25},{2,10},{10,18},{18,26},{... | collective-permute-start | bytes 12296 | tf_op jit(solution)/shard_map/ppermute | solution.py:15
  31.0 0.6 collective-permute-done.2
  32.7 0.8 multiply_reduce_fusion
  33.4 0.5 fusion.189
  34.8 1.3 collective-permute-start.4
  36.1 4.7 %collective-permute-start.7 = (bf16[1,16,256]{2,1,0:T(8,128)(2,1)S(1)}, bf16[1,16,256]{2,1,0:T(8,128)(2,1)S(1)}, u32[]{:S(2)}, u32[]{:S(2)}) collective-permute-start(bf16[1,16,256]{2,1,0:T(8,128)(2,1)S(1)} %slice.240), channel_id=1, source_target_pairs={{0,8},{8,16},{16,24},{1,9},{9,17},{17,25},{2,10},{10,18},{18,26},{... | collective-permute-start | bytes 24584 | tf_op jit(solution)/shard_map/ppermute | solution.py:15
  41.7 0.8 multiply_reduce_fusion.1
  42.5 0.4 fusion.188
  43.5 1.3 collective-permute-start.5
  45.4 2.9 %collective-permute-done.5 = bf16[1,4,256]{2,1,0:T(4,128)(2,1)S(1)} collective-permute-done((bf16[1,4,256]{2,1,0:T(4,128)(2,1)S(1)}, bf16[1,4,256]{2,1,0:T(4,128)(2,1)S(1)}, u32[]{:S(2)}, u32[]{:S(2)}) %collective-permute-start.5) | collective-permute-done | bytes 2080 | tf_op jit(solution)/shard_map/ppermute | solution.py:15
  48.6 0.8 multiply_reduce_fusion.2
  49.4 0.4 fusion.187
  51.3 2.1 pad_maximum_fusion
  53.4 0.6 copy-done.5
  54.0 1.2 sort.17
  55.2 0.7 gather_fusion
  55.9 0.7 reshape.430
  56.6 5.8 %all-to-all-start = ((s32[1,8,2]{2,0,1:T(1,128)}), s32[1,8,2]{2,0,1:T(1,128)S(1)}, u32[]{:S(2)}, u32[]{:S(2)}) async-start(s32[1,8,2]{2,0,1:T(1,128)} %bitcast.75), calls=%async_computation | async-start | bytes 8192 | tf_op jit(solution)/shard_map/all_to_all | solution.py:130
  62.4 0.6 gather_fusion.1
  63.1 0.7 fusion.162
  63.7 5.3 %all-to-all-done = s32[1,8,2]{2,0,1:T(1,128)S(1)} async-done(((s32[1,8,2]{2,0,1:T(1,128)}), s32[1,8,2]{2,0,1:T(1,128)S(1)}, u32[]{:S(2)}, u32[]{:S(2)}) %all-to-all-start) | async-done | bytes 96 | tf_op jit(solution)/shard_map/all_to_all | solution.py:130
  69.1 3.3 %all-to-all-start.1 = ((bf16[1,8,2,128]{3,2,0,1:T(2,128)(2,1)}), bf16[1,8,2,128]{3,2,0,1:T(2,128)(2,1)S(1)}, u32[]{:S(2)}, u32[]{:S(2)}) async-start(bf16[1,8,2,128]{3,2,0,1:T(2,128)(2,1)} %fusion.162), calls=%async_computation.1 | async-start | bytes 8192 | tf_op jit(solution)/shard_map/all_to_all | solution.py:129
  72.5 6.4 %all-to-all-done.1 = bf16[1,8,2,128]{3,2,0,1:T(2,128)(2,1)S(1)} async-done(((bf16[1,8,2,128]{3,2,0,1:T(2,128)(2,1)}), bf16[1,8,2,128]{3,2,0,1:T(2,128)(2,1)S(1)}, u32[]{:S(2)}, u32[]{:S(2)}) %all-to-all-start.1) | async-done | bytes 4128 | tf_op jit(solution)/shard_map/all_to_all | solution.py:129
  79.0 0.8 fusion.160
  79.7 1.3 collective-permute-start.6
  81.3 103.3 %all-reduce.5.cloned.1.call-done = f32[4,3,256,256]{3,2,1,0:T(8,128)} async-done(((f32[4,3,256,256]{3,2,1,0:T(8,128)}), f32[4,3,256,256]{3,2,1,0:T(8,128)}) %all-reduce.5.cloned.1.call-update) | async-done | bytes 3145744 | tf_op jit(solution)/shard_map/psum | solution.py:116
  185.0 0.8 fusion.29
  185.8 19.7 %all-reduce = (f32[4,256]{1,0:T(4,128)S(1)}, f32[4,256]{1,0:T(4,128)S(1)}) all-reduce(f32[4,256]{1,0:T(4,128)S(1)} %pad_maximum_fusion.8, f32[4,256]{1,0:T(4,128)S(1)} %pad_maximum_fusion.9), channel_id=1, replica_groups=mesh['seq'=4,'user'=8] {'user'}, use_global_device_ids=true, to_apply=%region_22.0 | all-reduce | flops 2048 | bytes 16384 | tf_op jit(solution)/shard_map/psum | solution.py:116
  205.4 6.8 %all-reduce.1 = (f32[4,256]{1,0:T(4,128)S(1)}, f32[4,256]{1,0:T(4,128)S(1)}) all-reduce(f32[4,256]{1,0:T(4,128)S(1)} %get-tuple-element.19, f32[4,256]{1,0:T(4,128)S(1)} %get-tuple-element.20), channel_id=1, replica_groups=mesh['seq'=4,'user'=8] {'seq'}, use_global_device_ids=true, to_apply=%region_23.0 | all-reduce | flops 2048 | bytes 16384 | tf_op jit(solution)/shard_map/psum | solution.py:115
  212.2 0.6 broadcast_multiply_fusion.2
  212.8 0.6 broadcast_multiply_fusion.1
  213.4 1.0 fusion.28
  214.5 40.3 %all-reduce.7.cloned.1.call-done = f32[4,3,256,256]{3,2,1,0:T(8,128)} async-done(((f32[4,3,256,256]{3,2,1,0:T(8,128)}), f32[4,3,256,256]{3,2,1,0:T(8,128)}) %all-reduce.7.cloned.1.call-update) | async-done | bytes 3145744 | tf_op jit(solution)/shard_map/psum | solution.py:115
  254.8 3.8 %broadcast_multiply_fusion = f32[4,3,256,256]{3,2,1,0:T(8,128)} fusion(f32[4,3,256,256]{3,2,1,0:T(8,128)} %all-reduce.7.cloned.1.call-done), kind=kLoop, calls=%fused_computation.3 | loop fusion | flops 786432 | bytes 6291456 | tf_op jit(solution)/shard_map/mul | solution.py:135
  (89 shorter events, 8.8 us)
Async XLA Ops:
  7.2 55.2 %copy-start = (bf16[1,16,128]{2,1,0:T(8,128)(2,1)S(1)}, bf16[1,16,128]{2,1,0:T(8,128)(2,1)}, u32[]{:S(2)}) copy-start(bf16[1,16,128]{2,1,0:T(8,128)(2,1)} %param.13) | copy-start | bytes 12292
  7.2 11.2 %copy-start.3 = (bf16[1,512,256]{2,1,0:T(8,128)(2,1)S(1)}, bf16[1,512,256]{2,1,0:T(8,128)(2,1)}, u32[]{:S(2)}) copy-start(bf16[1,512,256]{2,1,0:T(8,128)(2,1)} %param.9) | copy-start | bytes 786436
  7.2 11.0 %copy-start.4 = (bf16[4,3,256,256]{3,2,1,0:T(8,128)(2,1)S(1)}, bf16[4,3,256,256]{3,2,1,0:T(8,128)(2,1)}, u32[]{:S(2)}) copy-start(bf16[4,3,256,256]{3,2,1,0:T(8,128)(2,1)} %param.10) | copy-start | bytes 4718596
  7.2 177.4 %all-reduce.5.cloned.1.call-start = ((), (), s32[]{:S(2)}) async-start(), calls=%async_computation.2 | async-start | bytes 6291456 | tf_op jit(solution)/shard_map/psum | solution.py:116
  11.7 6.7 %collective-permute-start = (bf16[1,2,256]{2,1,0:T(2,128)(2,1)S(1)}, bf16[1,2,256]{2,1,0:T(2,128)(2,1)S(1)}, u32[]{:S(2)}, u32[]{:S(2)}) collective-permute-start(bf16[1,2,256]{2,1,0:T(2,128)(2,1)S(1)} %slice.220), channel_id=1, source_target_pairs={{0,8},{8,16},{16,24},{1,9},{9,17},{17,25},{2,10},{10,18},{18,26},{... | collective-permute-start | bytes 3080 | tf_op jit(solution)/shard_map/ppermute | solution.py:15
  14.8 17.6 %collective-permute-start.3 = (bf16[1,16,256]{2,1,0:T(8,128)(2,1)S(1)}, bf16[1,16,256]{2,1,0:T(8,128)(2,1)S(1)}, u32[]{:S(2)}, u32[]{:S(2)}) collective-permute-start(bf16[1,16,256]{2,1,0:T(8,128)(2,1)S(1)} %slice.198), channel_id=1, source_target_pairs={{8,0},{16,8},{24,16},{9,1},{17,9},{25,17},{10,2},{18,10},{26,18},{... | collective-permute-start | bytes 24584 | tf_op jit(solution)/shard_map/ppermute | solution.py:15
  18.1 1.0 copy-start.2
  20.0 6.0 %collective-permute-start.1 = (bf16[1,4,256]{2,1,0:T(4,128)(2,1)S(1)}, bf16[1,4,256]{2,1,0:T(4,128)(2,1)S(1)}, u32[]{:S(2)}, u32[]{:S(2)}) collective-permute-start(bf16[1,4,256]{2,1,0:T(4,128)(2,1)S(1)} %slice.223), channel_id=1, source_target_pairs={{0,8},{8,16},{16,24},{1,9},{9,17},{17,25},{2,10},{10,18},{18,26},{... | collective-permute-start | bytes 6152 | tf_op jit(solution)/shard_map/ppermute | solution.py:15
  27.2 4.4 %collective-permute-start.2 = (bf16[1,8,256]{2,1,0:T(8,128)(2,1)S(1)}, bf16[1,8,256]{2,1,0:T(8,128)(2,1)S(1)}, u32[]{:S(2)}, u32[]{:S(2)}) collective-permute-start(bf16[1,8,256]{2,1,0:T(8,128)(2,1)S(1)} %slice.226), channel_id=1, source_target_pairs={{0,8},{8,16},{16,24},{1,9},{9,17},{17,25},{2,10},{10,18},{18,26},{... | collective-permute-start | bytes 12296 | tf_op jit(solution)/shard_map/ppermute | solution.py:15
  34.8 6.7 %collective-permute-start.4 = (bf16[1,8,256]{2,1,0:T(8,128)(2,1)S(1)}, bf16[1,8,256]{2,1,0:T(8,128)(2,1)S(1)}, u32[]{:S(2)}, u32[]{:S(2)}) collective-permute-start(bf16[1,8,256]{2,1,0:T(8,128)(2,1)S(1)} %slice.231), channel_id=1, source_target_pairs={{8,0},{16,8},{24,16},{9,1},{17,9},{25,17},{10,2},{18,10},{26,18},{... | collective-permute-start | bytes 12296 | tf_op jit(solution)/shard_map/ppermute | solution.py:15
  36.1 14.6 %collective-permute-start.7 = (bf16[1,16,256]{2,1,0:T(8,128)(2,1)S(1)}, bf16[1,16,256]{2,1,0:T(8,128)(2,1)S(1)}, u32[]{:S(2)}, u32[]{:S(2)}) collective-permute-start(bf16[1,16,256]{2,1,0:T(8,128)(2,1)S(1)} %slice.240), channel_id=1, source_target_pairs={{0,8},{8,16},{16,24},{1,9},{9,17},{17,25},{2,10},{10,18},{18,26},{... | collective-permute-start | bytes 24584 | tf_op jit(solution)/shard_map/ppermute | solution.py:15
  43.5 4.8 %collective-permute-start.5 = (bf16[1,4,256]{2,1,0:T(4,128)(2,1)S(1)}, bf16[1,4,256]{2,1,0:T(4,128)(2,1)S(1)}, u32[]{:S(2)}, u32[]{:S(2)}) collective-permute-start(bf16[1,4,256]{2,1,0:T(4,128)(2,1)S(1)} %slice.234), channel_id=1, source_target_pairs={{8,0},{16,8},{24,16},{9,1},{17,9},{25,17},{10,2},{18,10},{26,18},{... | collective-permute-start | bytes 6152 | tf_op jit(solution)/shard_map/ppermute | solution.py:15
  53.3 0.7 copy-start.5
  53.3 1.9 copy-start.1
  56.6 12.5 %all-to-all-start = ((s32[1,8,2]{2,0,1:T(1,128)}), s32[1,8,2]{2,0,1:T(1,128)S(1)}, u32[]{:S(2)}, u32[]{:S(2)}) async-start(s32[1,8,2]{2,0,1:T(1,128)} %bitcast.75), calls=%async_computation | async-start | bytes 8192 | tf_op jit(solution)/shard_map/all_to_all | solution.py:130
  69.1 9.9 %all-to-all-start.1 = ((bf16[1,8,2,128]{3,2,0,1:T(2,128)(2,1)}), bf16[1,8,2,128]{3,2,0,1:T(2,128)(2,1)S(1)}, u32[]{:S(2)}, u32[]{:S(2)}) async-start(bf16[1,8,2,128]{3,2,0,1:T(2,128)(2,1)} %fusion.162), calls=%async_computation.1 | async-start | bytes 8192 | tf_op jit(solution)/shard_map/all_to_all | solution.py:129
  72.4 182.4 %all-reduce.7.cloned.1.call-start = ((), (), s32[]{:S(2)}) async-start(), calls=%async_computation.3 | async-start | bytes 6291456 | tf_op jit(solution)/shard_map/psum | solution.py:115
  79.7 104.9 %collective-permute-start.6 = (bf16[1,2,256]{2,1,0:T(2,128)(2,1)S(1)}, bf16[1,2,256]{2,1,0:T(2,128)(2,1)S(1)}, u32[]{:S(2)}, u32[]{:S(2)}) collective-permute-start(bf16[1,2,256]{2,1,0:T(2,128)(2,1)S(1)} %slice.237), channel_id=1, source_target_pairs={{8,0},{16,8},{24,16},{9,1},{17,9},{25,17},{10,2},{18,10},{26,18},{... | collective-permute-start | bytes 3080 | tf_op jit(solution)/shard_map/ppermute | solution.py:15
Sparse Core Ops, SparseCore 0:
  53.5 131.1 all-reduce.4
  187.0 67.7 all-reduce.6
